TPU v7x, 256 devices: a whole 4x4x8 slice. The times are simulated.
256 devices in a mesh: row: 32 (over y_lo, z, core), col: 8 (over x, y_hi).
Axes of the slice: x: 4, y: 4 (y_hi: 2, y_lo: 2; y = y_hi * 2 + y_lo), z: 8, core: 2. Of those that a mesh axis runs over, the one named last changes fastest.
Arguments:
- inverse_tiles: bfloat16 [128, 256, 128, 256], P('col', None, 'row'), may hold values from -6 to 6
- factor_panels: bfloat16 [2, 128, 256, 256], P(None, 'row', 'col'), may hold values from -0.0390625 to 0.0390625
- ancestors: int32 [2, 96], replicated, may hold values from 0 to 127, as said below
- valid_flags: int32 [2, 96], replicated, may hold values from 0 to 1, as said below
- block_slot: int32 [128], replicated, may hold values from 0 to 127, each once
Outputs:
- new_panels: float32 [128, 256, 2, 256], P('col', 'row')
Inputs may be any that keep to these rules, and one draw needn't show every extreme that they name: `ancestors`: within one supernode's list all 96 entries name different blocks. `valid_flags`: each list's used entries come first; supernode 0's list is used in full, the others in 64 entries or more.
All inputs are finite; a program needn't handle non-finite values.
Results may differ from a plain program's by a relative error of at most 0.0003.
Values may be sent and summed in bfloat16 or wider, within the bound.
No kernel may reach another device: no remote copies, remote signals or barrier semaphores. Data moves between devices by JAX's collectives and lax.ppermute only.
A program may use at most 64 MiB of HBM per device.

v0:
```python
import jax
import jax.numpy as jnp
from jax import lax
from jax.sharding import PartitionSpec as P


def membership(ancestors, valid_flags, block_slot):
    blocks = jnp.arange(block_slot.shape[0], dtype=jnp.int32)
    pick = (ancestors[:, :, None] == blocks[None, None, :]).astype(jnp.int32)
    slots = jnp.sum(pick * block_slot[None, None, :], axis=2)
    hits = (slots[:, :, None] == blocks[None, None, :]) & (valid_flags[:, :, None] == 1)
    return jnp.any(hits, axis=1)


def panel_product(left, right):
    return jnp.dot(left, right, preferred_element_type=jnp.float32)


def per_device(inverse_tiles, factor_panels, ancestors, valid_flags, block_slot):
    local_rows = inverse_tiles.shape[0]
    width = inverse_tiles.shape[1]
    local_cols = inverse_tiles.shape[2]
    panel_count = factor_panels.shape[0]
    member = membership(ancestors, valid_flags, block_slot)
    col_start = lax.axis_index("row") * local_cols
    row_start = lax.axis_index("col") * local_rows
    col_member = lax.dynamic_slice_in_dim(member, col_start, local_cols, 1)
    row_member = lax.dynamic_slice_in_dim(member, row_start, local_rows, 1)
    left = inverse_tiles.reshape(local_rows * width, local_cols * width)
    masked_local = jnp.where(
        col_member[:, :, None, None], factor_panels, jnp.zeros((), factor_panels.dtype)
    )
    results = []
    for which in range(panel_count):
        whole = lax.all_gather(masked_local[which], "col", axis=1, tiled=True)
        right = whole.reshape(local_cols * width, width)
        partial_value = panel_product(left, right)
        summed = lax.psum_scatter(
            partial_value.reshape(local_rows, width, width), "row", scatter_dimension=1, tiled=True
        )
        results.append(summed)
    stacked = jnp.stack(results, axis=2)
    rowmask = jnp.transpose(row_member)[:, None, :, None]
    return jnp.where(rowmask, -stacked, jnp.zeros((), jnp.float32))


def solution(mesh):
    return jax.shard_map(
        per_device,
        mesh=mesh,
        in_specs=(P("col", None, "row", None), P(None, "row", "col", None), P(), P(), P()),
        out_specs=P("col", "row", None, None),
        check_vma=False,
    )
```

profile of v0, /device:TPU:2, one launch (start us, length us, event | category | flops | bytes accessed | tf_op | source)
XLA Modules:
  0.0 325.4 jit_solution(16764533010754993528)
XLA Ops:
  6.5 0.0 reduce-scatter.3.cloned.1.call-start
  6.5 0.7 broadcast_compare_fusion
  7.2 0.9 select_reduce_fusion
  8.1 0.1 fusion.2
  8.2 0.1 constant_dynamic-slice_fusion
  8.3 1.0 broadcast_select_fusion
  9.3 34.7 %all-gather = bf16[1,4,256,256]{3,2,1,0:T(8,128)(2,1)S(1)} all-gather(bf16[1,4,32,256]{3,2,1,0:T(8,128)(2,1)S(1)} %get-tuple-element.5), channel_id=2, replica_groups=mesh['row'=32,'col'=8] {'col'}, dimensions={2}, use_global_device_ids=true | all-gather | bytes 589824 | tf_op jit(solution)/shard_map/all_gather | solution.py:35
  44.1 9.4 %copy.17 = bf16[512,8,4,256]{3,1,2,0:T(8,128)(2,1)} copy(bf16[512,8,4,256]{3,2,1,0:T(4,128)(2,1)} %bitcast.21) | data formatting | bytes 16777216
  53.4 7.8 %convolution_bitcast_fusion.1 = f32[4096,256]{0,1:T(8,128)} fusion(bf16[1024,256]{1,0:T(8,128)(2,1)S(1)} %bitcast.24, bf16[4096,1024]{1,0:T(8,128)(2,1)} %bitcast.22), kind=kOutput, calls=%fused_computation.1 | convolution fusion | flops 2147483648 | bytes 13107200 | tf_op jit(solution)/shard_map/dot_general | solution.py:16
  61.2 5.6 %copy.15 = f32[4096,256]{1,0:T(8,128)} copy(f32[4096,256]{0,1:T(8,128)} %convolution_bitcast_fusion.1) | data formatting | bytes 8388608 | tf_op jit(solution)/shard_map/reshape | solution.py:39
  66.8 0.0 reduce-scatter.3.cloned.1.call-update
  66.9 0.0 reduce-scatter.5.cloned.1.call-start
  66.9 35.3 %all-gather.1 = bf16[1,4,256,256]{3,2,1,0:T(8,128)(2,1)S(1)} all-gather(bf16[1,4,32,256]{3,2,1,0:T(8,128)(2,1)S(1)} %get-tuple-element.6), channel_id=3, replica_groups=mesh['row'=32,'col'=8] {'col'}, dimensions={2}, use_global_device_ids=true | all-gather | bytes 589824 | tf_op jit(solution)/shard_map/all_gather | solution.py:35
  102.2 7.8 %convolution_bitcast_fusion = f32[4096,256]{0,1:T(8,128)} fusion(bf16[1024,256]{1,0:T(8,128)(2,1)S(1)} %bitcast.25, bf16[4096,1024]{1,0:T(8,128)(2,1)} %bitcast.23), kind=kOutput, calls=%fused_computation | convolution fusion | flops 2147483648 | bytes 13107200 | tf_op jit(solution)/shard_map/dot_general | solution.py:16
  110.0 5.6 %copy.16 = f32[4096,256]{1,0:T(8,128)} copy(f32[4096,256]{0,1:T(8,128)} %convolution_bitcast_fusion) | data formatting | bytes 8388608 | tf_op jit(solution)/shard_map/reshape | solution.py:39
  115.6 0.0 reduce-scatter.5.cloned.1.call-update
  115.7 0.1 dynamic-slice_bitcast_fusion
  115.7 78.5 %reduce-scatter.3.cloned.1.call-done = f32[16,8,256]{2,1,0:T(8,128)} async-done(((f32[16,256,256]{2,1,0:T(8,128)}), f32[16,8,256]{2,1,0:T(8,128)}) %reduce-scatter.3.cloned.1.call-update) | async-done | bytes 131088 | tf_op jit(solution)/shard_map/reduce_scatter | solution.py:38
  194.3 122.3 %reduce-scatter.5.cloned.1.call-done = f32[16,8,256]{2,1,0:T(8,128)} async-done(((f32[16,256,256]{2,1,0:T(8,128)}), f32[16,8,256]{2,1,0:T(8,128)}) %reduce-scatter.5.cloned.1.call-update) | async-done | bytes 131088 | tf_op jit(solution)/shard_map/reduce_scatter | solution.py:38
  316.6 1.1 fusion
  317.6 0.9 copy.14
  (1 shorter events, 0.0 us)
Async XLA Ops:
  6.5 187.7 %reduce-scatter.3.cloned.1.call-start = ((), (), s32[]{:S(2)}) async-start(), calls=%async_computation.2 | async-start | bytes 4325376 | tf_op jit(solution)/shard_map/reduce_scatter | solution.py:38
  66.9 249.7 %reduce-scatter.5.cloned.1.call-start = ((), (), s32[]{:S(2)}) async-start(), calls=%async_computation.3 | async-start | bytes 4325376 | tf_op jit(solution)/shard_map/reduce_scatter | solution.py:38
Sparse Core Ops, SparseCore 0:
  67.0 127.2 reduce-scatter.2
  196.8 119.7 reduce-scatter.4
where the time goes:
time: 326 us; the launch traced here: 325 us
  waiting for transfers between devices  201 us (62%)
  blocking collectives  70.1 us (22%)
  local copies, waits for them, and re-layouts  21.6 us (7%)
  matrix products  15.6 us (5%)
  between operations  13.4 us (4%)
  other arithmetic  3.75 us (1%)
    reduce_scatter x2, waiting for transfers between devices, per_device(): lax.psum_scatter(partial_value.reshape(local_rows, width, width), 'row',...  201 us
    all_gather x2, blocking collectives, per_device(): whole = lax.all_gather(masked_local[which], 'col', axis=1, tiled=True)  70.1 us
    dot_general x2, matrix products, panel_product(): return jnp.dot(left, right, preferred_element_type=jnp.float32)  15.6 us
    reshape x2, local copies, waits for them, and re-layouts, per_device(): partial_value.reshape(local_rows, width, width)  11.2 us
    unnamed x1, local copies, waits for them, and re-layouts  9.35 us
  transfers between devices with their start and end apart: 2, of which 2 were waited for; matrix products, arithmetic and copies ran while one was open for 4% of the time, Pallas kernels for 0%

commit v1 on v0

--- a/solution.py
+++ b/solution.py
@@ -32,7 +32,10 @@
     )
     results = []
     for which in range(panel_count):
-        whole = lax.all_gather(masked_local[which], "col", axis=1, tiled=True)
+        whole = jnp.concatenate(
+            lax.all_to_all(jnp.stack([masked_local[which]] * lax.axis_size("col")), "col", 0, 0),
+            axis=1,
+        )
         right = whole.reshape(local_cols * width, width)
         partial_value = panel_product(left, right)
         summed = lax.psum_scatter(

time: 326 us -> 299 us (0.917)
  blocking collectives: 70.1 us -> 15.7 us
  waiting for transfers between devices: 201 us -> 220 us
  starting transfers between devices: 0.04 us -> 7.51 us
    all_gather x2 -> x0, blocking collectives: 70.1 us -> none  [per_device(): whole = lax.all_gather(masked_local[which], 'col', axis=1, tiled=True)]
    reduce_scatter x2, waiting for transfers between devices: 201 us -> 219 us  [per_device(): lax.psum_scatter(partial_value.reshape(local_rows, width, width), 'row',...]
    all_to_all x0 -> x1, blocking collectives: none -> 15.7 us  [per_device(): lax.all_to_all(jnp.stack([masked_local[which]] * lax.axis_size('col')), '...]
    all_to_all x0 -> x1, starting transfers between devices: none -> 7.46 us  [per_device(): lax.all_to_all(jnp.stack([masked_local[which]] * lax.axis_size('col')), '...]
  transfers between devices with their start and end apart: 2 -> 3, of which waited for: 2 -> 3; matrix products, arithmetic and copies ran while one was open for 4% -> 8% of each run, Pallas kernels for 0% -> 0%
where the time goes in v1:
time: 299 us; the launch traced here: 298 us
  waiting for transfers between devices  220 us (74%)
  local copies, waits for them, and re-layouts  22.7 us (8%)
  blocking collectives  15.7 us (5%)
  matrix products  15.5 us (5%)
  between operations  13.5 us (5%)
  starting transfers between devices  7.51 us (3%)
  other arithmetic  3.75 us (1%)
    reduce_scatter x2, waiting for transfers between devices, per_device(): lax.psum_scatter(partial_value.reshape(local_rows, width, width), 'row',...  219 us
    all_to_all x1, blocking collectives, per_device(): lax.all_to_all(jnp.stack([masked_local[which]] * lax.axis_size('col')), '...  15.7 us
    dot_general x2, matrix products, panel_product(): return jnp.dot(left, right, preferred_element_type=jnp.float32)  15.5 us
    reshape x2, local copies, waits for them, and re-layouts, per_device(): partial_value.reshape(local_rows, width, width)  11.2 us
    unnamed x1, local copies, waits for them, and re-layouts  9.35 us
    all_to_all x1, starting transfers between devices, per_device(): lax.all_to_all(jnp.stack([masked_local[which]] * lax.axis_size('col')), '...  7.46 us
  transfers between devices with their start and end apart: 3, of which 3 were waited for; matrix products, arithmetic and copies ran while one was open for 8% of the time, Pallas kernels for 0%

profile of v1, /device:TPU:2, one launch (start us, length us, event | category | flops | bytes accessed | tf_op | source)
XLA Modules:
  0.0 298.1 jit_solution(7570672549993864059)
XLA Ops:
  6.5 0.7 broadcast_compare_fusion
  7.2 0.9 select_reduce_fusion
  8.1 0.1 fusion.2
  8.2 0.1 constant_dynamic-slice_fusion
  8.3 1.0 broadcast_select_fusion
  9.3 0.9 stack.17
  10.2 7.5 %all-to-all-start.1 = ((bf16[8,4,32,256]{3,2,1,0:T(8,128)(2,1)}), bf16[8,4,32,256]{3,2,1,0:T(8,128)(2,1)S(1)}, u32[]{:S(2)}, u32[]{:S(2)}) async-start(bf16[8,4,32,256]{3,2,1,0:T(8,128)(2,1)} %stack.17), calls=%async_computation.2 | async-start | bytes 1048576 | tf_op jit(solution)/shard_map/all_to_all | solution.py:36
  17.7 0.0 reduce-scatter.5.cloned.1.call-start
  17.7 9.4 %copy.24 = bf16[512,8,4,256]{3,1,2,0:T(8,128)(2,1)} copy(bf16[512,8,4,256]{3,2,1,0:T(4,128)(2,1)} %bitcast.29) | data formatting | bytes 16777216
  27.0 0.3 all-to-all-done.1
  27.3 7.7 %convolution_bitcast_fusion = f32[4096,256]{0,1:T(8,128)} fusion(bf16[1024,256]{1,0:T(8,128)(2,1)S(1)} %bitcast.33, bf16[4096,1024]{1,0:T(8,128)(2,1)} %bitcast.30), kind=kOutput, calls=%fused_computation | convolution fusion | flops 2147483648 | bytes 13107200 | tf_op jit(solution)/shard_map/dot_general | solution.py:16
  35.1 5.6 %copy.23 = f32[4096,256]{1,0:T(8,128)} copy(f32[4096,256]{0,1:T(8,128)} %convolution_bitcast_fusion) | data formatting | bytes 8388608 | tf_op jit(solution)/shard_map/reshape | solution.py:42
  40.7 0.0 reduce-scatter.5.cloned.1.call-update
  40.7 0.0 reduce-scatter.3.cloned.1.call-start
  40.7 0.1 stack.15
  40.8 15.7 %all_to_all.10 = bf16[8,4,32,256]{3,2,1,0:T(8,128)(2,1)S(1)} all-to-all(bf16[8,4,32,256]{3,2,1,0:T(8,128)(2,1)S(1)} %stack.15), channel_id=1, replica_groups=mesh['row'=32,'col'=8] {'col'}, dimensions={0} | all-to-all | bytes 1048576 | tf_op jit(solution)/shard_map/all_to_all | solution.py:36
  56.5 7.7 %convolution_bitcast_fusion.1 = f32[4096,256]{0,1:T(8,128)} fusion(bf16[1024,256]{1,0:T(8,128)(2,1)S(1)} %bitcast.32, bf16[4096,1024]{1,0:T(8,128)(2,1)} %bitcast.31), kind=kOutput, calls=%fused_computation.1 | convolution fusion | flops 2147483648 | bytes 13107200 | tf_op jit(solution)/shard_map/dot_general | solution.py:16
  64.2 5.6 %copy.22 = f32[4096,256]{1,0:T(8,128)} copy(f32[4096,256]{0,1:T(8,128)} %convolution_bitcast_fusion.1) | data formatting | bytes 8388608 | tf_op jit(solution)/shard_map/reshape | solution.py:42
  69.8 0.0 reduce-scatter.3.cloned.1.call-update
  69.9 0.1 dynamic-slice_bitcast_fusion
  70.0 97.0 %reduce-scatter.5.cloned.1.call-done = f32[16,8,256]{2,1,0:T(8,128)} async-done(((f32[16,256,256]{2,1,0:T(8,128)}), f32[16,8,256]{2,1,0:T(8,128)}) %reduce-scatter.5.cloned.1.call-update) | async-done | bytes 131088 | tf_op jit(solution)/shard_map/reduce_scatter | solution.py:41
  166.9 122.3 %reduce-scatter.3.cloned.1.call-done = f32[16,8,256]{2,1,0:T(8,128)} async-done(((f32[16,256,256]{2,1,0:T(8,128)}), f32[16,8,256]{2,1,0:T(8,128)}) %reduce-scatter.3.cloned.1.call-update) | async-done | bytes 131088 | tf_op jit(solution)/shard_map/reduce_scatter | solution.py:41
  289.2 1.1 fusion
  290.3 0.9 copy.21
  (3 shorter events, 0.1 us)
Async XLA Ops:
  10.2 17.1 %all-to-all-start.1 = ((bf16[8,4,32,256]{3,2,1,0:T(8,128)(2,1)}), bf16[8,4,32,256]{3,2,1,0:T(8,128)(2,1)S(1)}, u32[]{:S(2)}, u32[]{:S(2)}) async-start(bf16[8,4,32,256]{3,2,1,0:T(8,128)(2,1)} %stack.17), calls=%async_computation.2 | async-start | bytes 1048576 | tf_op jit(solution)/shard_map/all_to_all | solution.py:36
  17.7 149.2 %reduce-scatter.5.cloned.1.call-start = ((), (), s32[]{:S(2)}) async-start(), calls=%async_computation.5 | async-start | bytes 4325376 | tf_op jit(solution)/shard_map/reduce_scatter | solution.py:41
  40.7 248.5 %reduce-scatter.3.cloned.1.call-start = ((), (), s32[]{:S(2)}) async-start(), calls=%async_computation.4 | async-start | bytes 4325376 | tf_op jit(solution)/shard_map/reduce_scatter | solution.py:41
Sparse Core Ops, SparseCore 0:
  40.8 126.0 reduce-scatter.4
  169.4 119.7 reduce-scatter.2
